TPU v7x, 32 devices: a whole 2x2x4 slice. The times are simulated.
32 devices in a mesh: pipe: 2 (over core), grp: 4 (over z), dp: 4 (over y, x).
Axes of the slice: x: 2, y: 2, z: 4, core: 2. Of those that a mesh axis runs over, the one named last changes fastest.
Arguments:
- block_input: bfloat16 [2, 16, 512, 512], P(None, ('grp', 'dp')), may hold values from -6 to 6
- cotangent: bfloat16 [2, 16, 512, 512], P(None, ('grp', 'dp')), may hold values from -6 to 6
- segments: int32 [2, 16, 512], P(None, ('grp', 'dp')), may hold values from 0 to 7, never falling along the last dimension, each value on 1 to 256 neighbouring positions
- ln1_gain: float32 [2, 512], P('pipe'), may hold values from 0.5 to 1.5
- ln1_shift: float32 [2, 512], P('pipe'), may hold values from -1.25 to 1.25
- qkv_weight: bfloat16 [2, 512, 1536], P('pipe'), may hold values from -0.25 to 0.25
- qkv_bias: float32 [2, 1536], P('pipe'), may hold values from -1.25 to 1.25
- attn_weight: bfloat16 [2, 512, 512], P('pipe'), may hold values from -1.5 to 1.5
- attn_bias: float32 [2, 512], P('pipe'), may hold values from -1.25 to 1.25
- ln2_gain: float32 [2, 512], P('pipe'), may hold values from 0.5 to 1.5
- ln2_shift: float32 [2, 512], P('pipe'), may hold values from -1.25 to 1.25
- ff_in_weight: bfloat16 [2, 512, 2048], P('pipe'), may hold values from -0.25 to 0.25
- ff_in_bias: float32 [2, 2048], P('pipe'), may hold values from -1.25 to 1.25
- ff_out_weight: bfloat16 [2, 2048, 512], P('pipe'), may hold values from -0.125 to 0.125
- ff_out_bias: float32 [2, 512], P('pipe'), may hold values from -1.25 to 1.25
- prefix_embed: float32 [10, 512], replicated, may hold values from -6 to 6
- up_weight: float32 [512, 512], replicated, may hold values from -0.25 to 0.25
- up_bias: float32 [512], replicated, may hold values from -3 to 3
- out_weight: float32 [512, 2048], replicated, may hold values from -0.375 to 0.375
- out_bias: float32 [2048], replicated, may hold values from -1.75 to 1.75
Outputs:
- activations: bfloat16 [2, 2, 16, 512, 512], P('pipe', None, ('grp', 'dp'))
- input_grads: float32 [2, 2, 16, 512, 512], P('pipe', None, ('grp', 'dp'))
- grad_embed: float32 [10, 512], replicated
- grad_up_weight: float32 [512, 512], replicated
- grad_up_bias: float32 [512], replicated
- grad_out_weight: float32 [512, 2048], P(None, ('pipe', 'dp'))
- grad_out_bias: float32 [2048], P(('pipe', 'dp'))
Inputs may be any that keep to these rules, and one draw needn't show every extreme that they name: `segments`: within a packed row segment numbers never fall, and every segment holds 1 to 256 tokens.
All inputs are finite; a program needn't handle non-finite values.
Results may differ from a plain program's by a relative error of at most 0.019.
Values may be sent and summed in bfloat16 or wider, within the bound.
No kernel may reach another device: no remote copies, remote signals or barrier semaphores. Data moves between devices by JAX's collectives and lax.ppermute only.
A program may use at most 192 MiB of HBM per device.

v0:
```python
from functools import partial
import math
import jax
import jax.numpy as jnp
from jax import lax
from jax.sharding import PartitionSpec as P

D = 512
HEADS = 8
HD = 64
FF = 2048
ROT = 16
PREFIX = 10


def passed_along(shard, axis, by):
    peers = lax.axis_size(axis)
    pairs = [(i, i + by) for i in range(peers) if 0 <= i + by < peers]
    return lax.ppermute(shard, axis, pairs)


def matmul_hi(left_mat, right_mat):
    return jnp.dot(
        left_mat, right_mat, precision=lax.Precision.HIGHEST, preferred_element_type=jnp.float32
    )


def layer_norm(values, gain_vec, shift_vec):
    row_mean = jnp.mean(values, axis=-1, keepdims=True)
    centered = values - row_mean
    variance = jnp.mean(centered * centered, axis=-1, keepdims=True)
    return centered * lax.rsqrt(variance + 1e-05) * gain_vec + shift_vec


def rotate_heads(head_rows):
    half_rot = ROT // 2
    positions = jnp.arange(head_rows.shape[0]).astype(head_rows.dtype)
    inv_freq = jnp.exp(
        jnp.arange(half_rot).astype(head_rows.dtype) * (-2.0 * math.log(10000.0) / ROT)
    )
    angles = positions[:, None] * inv_freq[None, :]
    cosine = jnp.cos(angles)[:, None, :]
    sine_val = jnp.sin(angles)[:, None, :]
    lead_part = head_rows[..., :half_rot]
    tail_part = head_rows[..., half_rot:ROT]
    return jnp.concatenate(
        [
            lead_part * cosine - tail_part * sine_val,
            tail_part * cosine + lead_part * sine_val,
            head_rows[..., ROT:],
        ],
        axis=-1,
    )


def block_mask(seg_row, row_start, block_rows):
    query_pos = row_start + jnp.arange(block_rows)
    key_pos = jnp.arange(seg_row.shape[0])
    seg_query = seg_row[row_start : row_start + block_rows]
    inner_mask = (key_pos[None, :] <= query_pos[:, None]) & (seg_row[None, :] == seg_query[:, None])
    return jnp.concatenate([jnp.ones((block_rows, PREFIX), dtype=jnp.bool_), inner_mask], axis=1)


def attention_forward(queries, key_list, value_list, seg_row):
    seq_len = queries.shape[0]
    block_rows = min(512, seq_len)
    scores = jnp.einsum(
        "qhd,khd->hqk", queries, key_list, preferred_element_type=jnp.float32
    ) * HD ** (-0.5)
    scores = jnp.where(block_mask(seg_row, 0, block_rows)[None], scores, -1e30)
    row_peak = jnp.max(scores, axis=-1, keepdims=True)
    exponent = jnp.exp(scores - row_peak)
    row_total = jnp.sum(exponent, axis=-1, keepdims=True)
    probs_low = (exponent / row_total).astype(jnp.bfloat16)
    outputs = [
        jnp.einsum(
            "hqk,khd->qhd", probs_low, value_list, preferred_element_type=jnp.float32
        ).astype(jnp.bfloat16)
    ]
    totals = [(row_peak + jnp.log(row_total))[..., 0]]
    return (jnp.concatenate(outputs, axis=0), jnp.concatenate(totals, axis=1))


def attention_backward(queries, key_list, value_list, log_totals, grad_mixed, seg_row):
    seq_len = queries.shape[0]
    block_rows = min(512, seq_len)
    grad_keys = jnp.zeros(key_list.shape, jnp.float32)
    grad_values = jnp.zeros(value_list.shape, jnp.float32)
    grad_query_parts = []
    for row_start in range(0, seq_len, block_rows):
        query_block = queries[row_start : row_start + block_rows]
        grad_block = grad_mixed[row_start : row_start + block_rows]
        allowed = block_mask(seg_row, row_start, block_rows)[None]
        scores = jnp.einsum(
            "qhd,khd->hqk", query_block, key_list, preferred_element_type=jnp.float32
        ) * HD ** (-0.5)
        block_lse = log_totals[:, row_start : row_start + block_rows][:, :, None]
        probs_full = jnp.where(allowed, jnp.exp(scores - block_lse), 0.0)
        probs_low = probs_full.astype(jnp.bfloat16)
        grad_values = grad_values + jnp.einsum(
            "hqk,qhd->khd", probs_low, grad_block, preferred_element_type=jnp.float32
        )
        grad_probs = jnp.einsum(
            "qhd,khd->hqk", grad_block, value_list, preferred_element_type=jnp.float32
        )
        inner_sum = jnp.sum(probs_full * grad_probs, axis=-1, keepdims=True)
        grad_scores = (probs_full * (grad_probs - inner_sum)).astype(jnp.bfloat16)
        grad_query_parts.append(
            jnp.einsum("hqk,khd->qhd", grad_scores, key_list, preferred_element_type=jnp.float32)
            * HD ** (-0.5)
        )
        grad_keys = grad_keys + jnp.einsum(
            "hqk,qhd->khd", grad_scores, query_block, preferred_element_type=jnp.float32
        ) * HD ** (-0.5)
    return (jnp.concatenate(grad_query_parts, axis=0), grad_keys, grad_values)


def forward_layer(row_in, seg_row, prefix_keys, prefix_values, params):
    (
        gain_one,
        shift_one,
        w_qkv,
        b_qkv,
        w_attn,
        b_attn,
        gain_two,
        shift_two,
        w_in,
        bias_in,
        w_back,
        bias_back,
    ) = params
    seq_len = row_in.shape[0]
    hidden = row_in.astype(jnp.float32)
    normed_one = layer_norm(hidden, gain_one, shift_one).astype(jnp.bfloat16)
    packed = jnp.dot(normed_one, w_qkv, preferred_element_type=jnp.float32) + b_qkv
    queries = rotate_heads(packed[:, :D].reshape(seq_len, HEADS, HD)).astype(jnp.bfloat16)
    key_rows = rotate_heads(packed[:, D : 2 * D].reshape(seq_len, HEADS, HD)).astype(jnp.bfloat16)
    value_rows = packed[:, 2 * D :].reshape(seq_len, HEADS, HD).astype(jnp.bfloat16)
    key_list = jnp.concatenate([prefix_keys, key_rows], axis=0)
    value_list = jnp.concatenate([prefix_values, value_rows], axis=0)
    mixed_heads, log_totals = attention_forward(queries, key_list, value_list, seg_row)
    attn_out = (
        jnp.dot(mixed_heads.reshape(seq_len, D), w_attn, preferred_element_type=jnp.float32)
        + b_attn
    )
    normed_two = layer_norm(hidden, gain_two, shift_two).astype(jnp.bfloat16)
    before = jnp.dot(normed_two, w_in, preferred_element_type=jnp.float32) + bias_in
    activated = jax.nn.gelu(before, approximate=False).astype(jnp.bfloat16)
    result = (
        hidden
        + attn_out
        + jnp.dot(activated, w_back, preferred_element_type=jnp.float32)
        + bias_back
    )
    return (result.astype(jnp.bfloat16), (queries, key_rows, value_rows, log_totals, before))


def backward_layer(grad_out, row_in, seg_row, prefix_keys, prefix_values, kept_state, params):
    (
        gain_one,
        shift_one,
        w_qkv,
        b_qkv,
        w_attn,
        b_attn,
        gain_two,
        shift_two,
        w_in,
        bias_in,
        w_back,
        bias_back,
    ) = params
    queries, key_rows, value_rows, log_totals, before = kept_state
    seq_len = row_in.shape[0]
    hidden = row_in.astype(jnp.float32)
    grad_activated = jnp.dot(grad_out, w_back.T, preferred_element_type=jnp.float32)
    gelu_back = jax.vjp(partial(jax.nn.gelu, approximate=False), before)[1]
    grad_before = gelu_back(grad_activated)[0].astype(jnp.bfloat16)
    grad_normed_two = jnp.dot(grad_before, w_in.T, preferred_element_type=jnp.float32)
    norm_two_back = jax.vjp(partial(layer_norm, gain_vec=gain_two, shift_vec=shift_two), hidden)[1]
    grad_mixed = (
        jnp.dot(grad_out, w_attn.T, preferred_element_type=jnp.float32)
        .astype(jnp.bfloat16)
        .reshape(seq_len, HEADS, HD)
    )
    key_list = jnp.concatenate([prefix_keys, key_rows], axis=0)
    value_list = jnp.concatenate([prefix_values, value_rows], axis=0)
    grad_queries, grad_keys, grad_values = attention_backward(
        queries, key_list, value_list, log_totals, grad_mixed, seg_row
    )
    grad_q_raw = jax.vjp(rotate_heads, grad_queries)[1](grad_queries)[0]
    grad_key_part = grad_keys[PREFIX:]
    grad_k_raw = jax.vjp(rotate_heads, grad_key_part)[1](grad_key_part)[0]
    grad_packed = jnp.concatenate(
        [
            grad_q_raw.reshape(seq_len, D),
            grad_k_raw.reshape(seq_len, D),
            grad_values[PREFIX:].reshape(seq_len, D),
        ],
        axis=1,
    ).astype(jnp.bfloat16)
    grad_normed_one = jnp.dot(grad_packed, w_qkv.T, preferred_element_type=jnp.float32)
    norm_one_back = jax.vjp(partial(layer_norm, gain_vec=gain_one, shift_vec=shift_one), hidden)[1]
    grad_in = (
        grad_out.astype(jnp.float32)
        + norm_two_back(grad_normed_two)[0]
        + norm_one_back(grad_normed_one)[0]
    )
    prefix_grad = jnp.concatenate(
        [grad_keys[:PREFIX].reshape(PREFIX, D), grad_values[:PREFIX].reshape(PREFIX, D)], axis=1
    )
    return (grad_in, prefix_grad)


def local(
    block_input,
    cotangent,
    segments,
    ln1_gain,
    ln1_shift,
    qkv_weight,
    qkv_bias,
    attn_weight,
    attn_bias,
    ln2_gain,
    ln2_shift,
    ff_in_weight,
    ff_in_bias,
    ff_out_weight,
    ff_out_bias,
    prefix_embed,
    up_weight,
    up_bias,
    out_weight,
    out_bias,
):
    section_id = lax.axis_index("pipe")
    micro_count = block_input.shape[0]
    seq_len = block_input.shape[2]
    hidden_units = jnp.tanh(matmul_hi(prefix_embed, up_weight) + up_bias)
    prefix_states = matmul_hi(hidden_units, out_weight) + out_bias
    seg_rows = segments[:, 0]
    params = tuple(
        (
            array_in[0]
            for array_in in (
                ln1_gain,
                ln1_shift,
                qkv_weight,
                qkv_bias,
                attn_weight,
                attn_bias,
                ln2_gain,
                ln2_shift,
                ff_in_weight,
                ff_in_bias,
                ff_out_weight,
                ff_out_bias,
            )
        )
    )
    section_states = lax.dynamic_slice_in_dim(prefix_states, section_id * (2 * D), 2 * D, 1).astype(
        jnp.bfloat16
    )
    prefix_keys = section_states[:, :D].reshape(PREFIX, HEADS, HD)
    prefix_values = section_states[:, D:].reshape(PREFIX, HEADS, HD)

    def run_full(row_in, seg_row):
        return forward_layer(row_in, seg_row, prefix_keys, prefix_values, params)

    def skip_full(row_in, seg_row):
        return (
            jnp.zeros((seq_len, D), jnp.bfloat16),
            (
                jnp.zeros((seq_len, HEADS, HD), jnp.bfloat16),
                jnp.zeros((seq_len, HEADS, HD), jnp.bfloat16),
                jnp.zeros((seq_len, HEADS, HD), jnp.bfloat16),
                jnp.zeros((HEADS, seq_len), jnp.float32),
                jnp.zeros((seq_len, FF), jnp.float32),
            ),
        )

    received = jnp.zeros((seq_len, D), jnp.bfloat16)
    tick_inputs = []
    tick_outputs = []
    tick_kept = []
    for tick_num in range(micro_count + 1):
        micro_idx = tick_num - section_id
        active = (micro_idx >= 0) & (micro_idx < micro_count)
        clamped = jnp.clip(micro_idx, 0, micro_count - 1)
        own_row = block_input[min(tick_num, micro_count - 1), 0]
        row_in = jnp.where(section_id == 0, own_row, received)
        seg_row = lax.dynamic_index_in_dim(seg_rows, clamped, 0, keepdims=False)
        result, kept_state = lax.cond(active, run_full, skip_full, row_in, seg_row)
        tick_kept.append(kept_state)
        tick_inputs.append(row_in)
        tick_outputs.append(result)
        if tick_num < micro_count:
            received = passed_along(result, "pipe", 1)

    def by_section(early_val, later_val):
        return jnp.where(section_id == 0, early_val, later_val)

    inputs_by_micro = jnp.stack(
        [
            by_section(tick_inputs[micro_num], tick_inputs[micro_num + 1])
            for micro_num in range(micro_count)
        ]
    )
    outputs_by_micro = jnp.stack(
        [
            by_section(tick_outputs[micro_num], tick_outputs[micro_num + 1])
            for micro_num in range(micro_count)
        ]
    )
    kept_by_micro = jax.tree.map(
        lambda *leaf_list: jnp.stack(leaf_list),
        *[
            jax.tree.map(by_section, tick_kept[micro_num], tick_kept[micro_num + 1])
            for micro_num in range(micro_count)
        ]
    )

    def back_kept(grad_out, row_in, seg_row, kept_state):
        return backward_layer(
            grad_out, row_in, seg_row, prefix_keys, prefix_values, kept_state, params
        )

    def skip_kept(grad_out, row_in, seg_row, kept_state):
        return (jnp.zeros((seq_len, D), jnp.float32), jnp.zeros((PREFIX, 2 * D), jnp.float32))

    received_grad = jnp.zeros((seq_len, D), jnp.bfloat16)
    prefix_total = jnp.zeros((PREFIX, 2 * D), jnp.float32)
    tick_grads = []
    for tick_num in range(micro_count + 1):
        micro_idx = tick_num - 1 + section_id
        active = (micro_idx >= 0) & (micro_idx < micro_count)
        clamped = jnp.clip(micro_idx, 0, micro_count - 1)
        own_cot = cotangent[min(tick_num, micro_count - 1), 0]
        grad_out = jnp.where(section_id == 1, own_cot, received_grad)
        row_in = lax.dynamic_index_in_dim(inputs_by_micro, clamped, 0, keepdims=False)
        seg_row = lax.dynamic_index_in_dim(seg_rows, clamped, 0, keepdims=False)
        kept_state = jax.tree.map(
            partial(lax.dynamic_index_in_dim, index=clamped, axis=0, keepdims=False), kept_by_micro
        )
        grad_in, prefix_grad = lax.cond(
            active, back_kept, skip_kept, grad_out, row_in, seg_row, kept_state
        )
        prefix_total = prefix_total + prefix_grad
        tick_grads.append(grad_in)
        if tick_num < micro_count:
            received_grad = passed_along(grad_in.astype(jnp.bfloat16), "pipe", -1)
    grads_by_micro = jnp.stack(
        [
            jnp.where(section_id == 1, tick_grads[micro_num], tick_grads[micro_num + 1])
            for micro_num in range(micro_count)
        ]
    )
    dp_index = lax.axis_index("dp")
    col_width = 2 * D // lax.axis_size("dp")
    local_cols = lax.psum_scatter(prefix_total, "dp", scatter_dimension=1, tiled=True)
    local_cols = lax.psum(local_cols, "grp")
    grad_out_weight = matmul_hi(hidden_units.T, local_cols)
    grad_out_bias = jnp.sum(local_cols, axis=0)
    out_cols = lax.dynamic_slice_in_dim(
        out_weight, section_id * (2 * D) + dp_index * col_width, col_width, 1
    )
    hidden_part = matmul_hi(local_cols, out_cols.T)
    hidden_grad = lax.psum(hidden_part, ("pipe", "dp"))
    grad_pre = hidden_grad * (1.0 - hidden_units * hidden_units)
    grad_up_weight = matmul_hi(prefix_embed.T, grad_pre)
    grad_up_bias = jnp.sum(grad_pre, axis=0)
    grad_embed = matmul_hi(grad_pre, up_weight.T)
    activations = outputs_by_micro[None, :, None]
    input_grads = grads_by_micro[None, :, None]
    return (
        activations,
        input_grads,
        grad_embed,
        grad_up_weight,
        grad_up_bias,
        grad_out_weight,
        grad_out_bias,
    )


def solution(mesh):
    return jax.shard_map(
        local,
        mesh=mesh,
        in_specs=(
            P(None, ("grp", "dp"), None, None),
            P(None, ("grp", "dp"), None, None),
            P(None, ("grp", "dp"), None),
            P("pipe", None),
            P("pipe", None),
            P("pipe", None, None),
            P("pipe", None),
            P("pipe", None, None),
            P("pipe", None),
            P("pipe", None),
            P("pipe", None),
            P("pipe", None, None),
            P("pipe", None),
            P("pipe", None, None),
            P("pipe", None),
            P(),
            P(),
            P(),
            P(),
            P(),
        ),
        out_specs=(
            P("pipe", None, ("grp", "dp"), None, None),
            P("pipe", None, ("grp", "dp"), None, None),
            P(),
            P(),
            P(),
            P(None, ("pipe", "dp")),
            P(("pipe", "dp")),
        ),
        check_vma=False,
    )
```

profile of v0, /device:TPU:1, one launch (start us, length us, event | category | flops | bytes accessed | tf_op | source)
XLA Modules:
  0.0 516.9 jit_solution(15525232900893411581)
XLA Ops:
  10.4 4.3 fusion.604
  16.2 14.4 %conditional.6 = (bf16[512,512]{1,0:T(8,128)(2,1)}, bf16[512,8,64]{0,2,1:T(8,128)(2,1)}, bf16[512,8,64]{0,2,1:T(8,128)(2,1)}, bf16[512,8,64]{0,2,1:T(8,128)(2,1)...) conditional(s32[]{:T(128)} %convert_element_type.537, () %tuple.74, (bf16[512,512]{1,0:T(8,128)(2,1)S(1)}, ...), branch_computations={%region_0.1_spmd, %region_1.6_spmd} | conditional | flops 3878450176 | bytes 134584976 | solution.py:295
  16.2 2.5 broadcast.1317
  31.9 41.8 %collective-permute-done = bf16[512,512]{1,0:T(8,128)(2,1)} collective-permute-done((bf16[512,512]{1,0:T(8,128)(2,1)}, bf16[512,512]{1,0:T(8,128)(2,1)}, u32[]{:S(2)}, u32[]{:S(2)}) %collective-permute-start) | collective-permute-done | bytes 524320 | tf_op jit(solution)/shard_map/ppermute | solution.py:19
  75.6 54.4 %conditional.7 = (bf16[512,512]{1,0:T(8,128)(2,1)}, bf16[512,8,64]{0,2,1:T(8,128)(2,1)}, bf16[512,8,64]{0,2,1:T(8,128)(2,1)}, bf16[512,8,64]{0,2,1:T(8,128)(2,1)...) conditional(s32[]{:T(128)} %convert_element_type.539, () %tuple.76, (bf16[512,512]{1,0:T(8,128)(2,1)S(1)}, ...), branch_computations={%region_6.7_spmd, %region_7.12_spmd} | conditional | flops 3878450176 | bytes 134601392 | solution.py:295
  76.8 2.5 convolution_add_fusion.3
  82.5 2.5 copy.118
  85.0 2.5 copy.119
  95.1 3.6 fusion.419
  107.8 6.5 %fusion.437 = bf16[8,64,512]{2,1,0:T(8,128)(2,1)S(1)} fusion(f32[8,512,522]{1,2,0:T(8,128)} %copy-done.4, f32[8,512]{1,0:T(8,128)S(1)} %fusion.420, f32[8,512]{1,0:T(8,128)S(1)} %get-tuple-element.1338, pred[512,522]{0,1:T(8,128)(4,1)S(1)} %copy-done.32, bf16[512,8,64]{0,2,1:T(8,128)(2,1)} %bitcast.15, bf16[10,8,64]{0,2,1:T(8,128)(2,1)} %copy.131), kind=kOutput, calls=%fused_computation.587 | convolution fusion | flops 285700096 | bytes 9911296 | tf_op jit(solution)/shard_map/cond/branch_1_fun/hqk,khd->qhd/dot_general | solution.py:76
  114.3 3.5 convolution_add_fusion.4
  117.8 10.9 %fusion.432 = f32[512,512]{1,0:T(8,128)S(1)} fusion(bf16[2048,512]{1,0:T(8,128)(2,1)S(1)} %copy-done.71, f32[512,2048]{1,0:T(8,128)} %convolution_add_fusion.4), kind=kOutput, calls=%fused_computation.579 | convolution fusion | flops 1141899264 | bytes 7340032 | tf_op jit(solution)/shard_map/cond/branch_1_fun/dot_general | solution.py:153
  131.3 2.8 collective-permute-done.1
  136.1 47.9 %conditional.8 = (bf16[512,512]{1,0:T(8,128)(2,1)}, bf16[512,8,64]{0,2,1:T(8,128)(2,1)}, bf16[512,8,64]{0,2,1:T(8,128)(2,1)}, bf16[512,8,64]{0,2,1:T(8,128)(2,1)...) conditional(s32[]{:T(128)} %convert_element_type.540, () %tuple.78, (bf16[512,512]{1,0:T(8,128)(2,1)S(1)}, ...), branch_computations={%region_12.13_spmd, %region_13.18_spmd} | conditional | flops 3878450176 | bytes 134044168 | solution.py:295
  137.7 2.5 convolution_add_fusion.6
  143.1 2.5 copy.121
  152.3 3.4 fusion.503
  161.7 6.4 %fusion.521 = bf16[8,64,512]{2,1,0:T(8,128)(2,1)S(1)} fusion(f32[8,512,522]{1,2,0:T(8,128)} %copy-done.5, f32[8,512]{1,0:T(8,128)S(1)} %fusion.504, f32[8,512]{1,0:T(8,128)S(1)} %get-tuple-element.1352, pred[512,522]{0,1:T(8,128)(4,1)S(1)} %concatenate.116, bf16[512,8,64]{0,2,1:T(8,128)(2,1)} %bitcast.28, bf16[10,8,64]{0,2,1:T(8,128)(2,1)S(1)} %copy.133), kind=kOutput, calls=%fused_computation.704 | convolution fusion | flops 285700096 | bytes 9911296 | tf_op jit(solution)/shard_map/cond/branch_1_fun/hqk,khd->qhd/dot_general | solution.py:76
  168.2 3.4 convolution_add_fusion.7
  171.6 10.9 %fusion.516 = f32[512,512]{1,0:T(8,128)S(1)} fusion(bf16[2048,512]{1,0:T(8,128)(2,1)S(1)} %copy-done.72, f32[512,2048]{1,0:T(8,128)} %convolution_add_fusion.7), kind=kOutput, calls=%fused_computation.696 | convolution fusion | flops 1141899264 | bytes 7340032 | tf_op jit(solution)/shard_map/cond/branch_1_fun/dot_general | solution.py:153
  190.0 4.8 select_bitcast_fusion.1
  194.8 3.9 pad_maximum_fusion.18
  199.6 75.5 %conditional.9 = (f32[512,512]{0,1:T(8,128)}, f32[10,1024]{1,0:T(8,128)}) conditional(s32[]{:T(128)} %convert_element_type.541, () %tuple.80, (bf16[2,1,512,512]{3,2,1,0:T(8,128)(2,1)}, pred[512,512]{1,0:T(32,128)(4,1)}, bf16[]{:T(256)}, s32[]{:T(128)}, f32[2,512,2048]{2,1,0:T(8,128)}, /*index=5*/bf16[2048,512]{1,0:T(8,128)(2,1)}, ...), branch_computations={%region_18.19_spmd, %region_19.27_spmd} | conditional | flops 4719746048 | bytes 179329520 | solution.py:347
  202.1 6.8 %fusion.63 = f32[8,512,522]{1,2,0:T(8,128)} fusion(bf16[2,512,8,64]{1,3,2,0:T(8,128)(2,1)S(1)} %get-tuple-element.782, s32[]{:T(128)S(6)} %min.25, bf16[512,8,64]{0,2,1:T(8,128)(2,1)} %get-tuple-element.1281, bf16[10,8,64]{0,2,1:T(8,128)(2,1)S(1)} %copy.138), kind=kOutput, calls=%fused_computation.79 | convolution fusion | flops 274747392 | bytes 9732100 | tf_op jit(solution)/shard_map/cond/branch_1_fun/qhd,khd->hqk/dot_general | solution.py:94
  210.0 2.6 copy.135
  213.9 2.6 convolution_convert_fusion
  218.0 7.1 %multiply_reduce_fusion = (f32[8,512]{1,0:T(8,128)S(1)}, f32[8,512,522]{1,2,0:T(8,128)S(1)}) fusion(f32[8,512,522]{1,2,0:T(8,128)} %fusion.63, f32[8,512]{1,0:T(8,128)S(1)} %dynamic-slice_bitcast_fusion.2, pred[512,522]{0,1:T(8,128)(4,1)} %concatenate.121, bf16[512,8,64]{0,2,1:T(8,128)(2,1)} %bitcast.622, bf16[512,8,64]{0,2,1:T(8,128)(2,1)} %get-tuple-element.1280, ...), kind=kOutput, calls=%fused_computation.1 | convolution fusion | flops 285433856 | bytes 18463744 | tf_op jit(solution)/shard_map/cond/branch_1_fun/qhd,khd->hqk/dot_general | solution.py:103
  225.2 2.7 multiply_convert_fusion
  233.3 5.4 %fusion.37 = f32[522,8,64]{0,2,1:T(8,128)S(1)} fusion(bf16[512,8,64]{0,2,1:T(8,128)(2,1)} %bitcast.623, f32[8,512,522]{1,2,0:T(8,128)} %fusion.63, f32[8,512]{1,0:T(8,128)S(1)} %dynamic-slice_bitcast_fusion.2, pred[512,522]{0,1:T(8,128)(4,1)} %concatenate.121), kind=kOutput, calls=%fused_computation.48 | convolution fusion | flops 282230784 | bytes 10429440 | tf_op jit(solution)/shard_map/cond/branch_1_fun/hqk,qhd->khd/dot_general | solution.py:100
  242.0 3.4 fusion.40
  252.8 16.5 %fusion.54 = (f32[512]{0:T(512)S(1)}, f32[512]{0:T(512)S(1)}, f32[512]{0:T(512)S(1)}, f32[512,512]{0,1:T(8,128)}) fusion(f32[512]{0:T(512)S(1)} %broadcast_multiply_fusion, bf16[2,512,512]{1,2,0:T(8,128)(2,1)} %copy.137, s32[]{:T(128)S(6)} %min.25, f32[512,512]{0,1:T(8,128)} %fusion.41, f32[512]{0:T(512)S(1)} %bitcast.681, ...), kind=kOutput, calls=%fused_computation.63 | convolution fusion | flops 2225601024 | bytes 11808256 | tf_op jit(solution)/shard_map/cond/branch_1_fun/dot_general | solution.py:180
  271.5 3.4 add_add_fusion.2
  283.3 75.2 %conditional.10 = (f32[512,512]{0,1:T(8,128)}, f32[10,1024]{1,0:T(8,128)}) conditional(s32[]{:T(128)} %convert_element_type.542, () %tuple.82, (pred[512,512]{1,0:T(32,128)(4,1)}, bf16[512,512]{0,1:T(8,128)(2,1)}, bf16[512,512]{0,1:T(8,128)(2,1)}, s32[]{:T(128)}, f32[2,512,2048]{2,1,0:T(8,128)}, /*index=5*/bf16[2048,512]{1,0:T(8,128)(2,1)}, ...), branch_computations={%region_27.28_spmd, %region_28.36_spmd} | conditional | flops 4719221760 | bytes 178427408 | solution.py:347
  286.5 6.8 %fusion.179 = f32[8,512,522]{1,2,0:T(8,128)} fusion(bf16[2,512,8,64]{1,3,2,0:T(8,128)(2,1)S(1)} %get-tuple-element.801, s32[]{:T(128)S(6)} %min.26, bf16[512,8,64]{0,2,1:T(8,128)(2,1)} %get-tuple-element.1297, bf16[10,8,64]{0,2,1:T(8,128)(2,1)S(1)} %copy.143), kind=kOutput, calls=%fused_computation.224 | convolution fusion | flops 274747392 | bytes 9732100 | tf_op jit(solution)/shard_map/cond/branch_1_fun/qhd,khd->hqk/dot_general | solution.py:94
  297.1 2.5 convolution_convert_fusion.1
  301.2 7.1 %multiply_reduce_fusion.1 = (f32[8,512]{1,0:T(8,128)S(1)}, f32[8,512,522]{1,2,0:T(8,128)S(1)}) fusion(f32[8,512,522]{1,2,0:T(8,128)} %fusion.179, f32[8,512]{1,0:T(8,128)S(1)} %dynamic-slice_bitcast_fusion.5, pred[512,522]{0,1:T(8,128)(4,1)} %concatenate.126, bf16[512,8,64]{0,2,1:T(8,128)(2,1)} %bitcast.615, bf16[512,8,64]{0,2,1:T(8,128)(2,1)} %get-tuple-element.1296, ...), kind=kOutput, calls=%fused_computation.148 | convolution fusion | flops 285433856 | bytes 18463744 | tf_op jit(solution)/shard_map/cond/branch_1_fun/qhd,khd->hqk/dot_general | solution.py:103
  308.3 2.9 multiply_convert_fusion.1
  316.7 5.5 %fusion.154 = f32[522,8,64]{0,2,1:T(8,128)S(1)} fusion(bf16[512,8,64]{0,2,1:T(8,128)(2,1)} %bitcast.616, f32[8,512,522]{1,2,0:T(8,128)} %fusion.179, f32[8,512]{1,0:T(8,128)S(1)} %dynamic-slice_bitcast_fusion.5, pred[512,522]{0,1:T(8,128)(4,1)} %concatenate.126), kind=kOutput, calls=%fused_computation.195 | convolution fusion | flops 282230784 | bytes 10429440 | tf_op jit(solution)/shard_map/cond/branch_1_fun/hqk,qhd->khd/dot_general | solution.py:100
  325.5 3.4 fusion.157
  336.1 16.5 %fusion.171 = (f32[512]{0:T(512)S(1)}, f32[512]{0:T(512)S(1)}, f32[512]{0:T(512)S(1)}, f32[512,512]{0,1:T(8,128)}) fusion(f32[512]{0:T(512)S(1)} %broadcast_multiply_fusion.1, bf16[2,512,512]{1,2,0:T(8,128)(2,1)} %copy.142, s32[]{:T(128)S(6)} %min.26, f32[512,512]{0,1:T(8,128)} %fusion.158, f32[512]{0:T(512)S(1)} %bitcast.682, ...), kind=kOutput, calls=%fused_computation.210 | convolution fusion | flops 2225338880 | bytes 11545600 | tf_op jit(solution)/shard_map/cond/branch_1_fun/dot_general | solution.py:180
  352.6 2.6 fusion.181
  355.2 3.3 add_add_fusion.5
  362.7 2.6 copy.145
  367.7 2.5 copy.146
  370.2 4.6 conditional.11
  379.8 75.0 %reduce-scatter.2.cloned.1.call-done = f32[10,256]{1,0:T(8,128)} async-done(((f32[10,1024]{1,0:T(8,128)}), f32[10,256]{1,0:T(8,128)}) %reduce-scatter.2.cloned.1.call-update) | async-done | bytes 10256 | tf_op jit(solution)/shard_map/reduce_scatter | solution.py:362
  454.7 15.6 %psum.14 = f32[10,256]{1,0:T(8,128)S(1)} all-reduce(f32[10,256]{1,0:T(8,128)} %reduce-scatter.2.cloned.1.call-done), channel_id=1, replica_groups=mesh['pipe'=2,'grp'=4,'dp'=4] {'grp'}, use_global_device_ids=true, to_apply=%region_46.47 | all-reduce | flops 2560 | bytes 20480 | tf_op jit(solution)/shard_map/psum | solution.py:363
  473.3 31.4 %psum.15 = f32[10,512]{1,0:T(8,128)S(1)} all-reduce(f32[10,512]{1,0:T(8,128)S(1)} %fusion.588), channel_id=1, replica_groups=mesh['pipe'=2,'grp'=4,'dp'=4] {'pipe','dp'}, use_global_device_ids=true, to_apply=%region_47.48 | all-reduce | flops 5120 | bytes 40960 | tf_op jit(solution)/shard_map/psum | solution.py:370
  (315 shorter events, 139.7 us)
Async XLA Ops:
  7.2 8.9 %copy-start.15 = (bf16[2,1,512,512]{3,2,1,0:T(8,128)(2,1)S(1)}, bf16[2,1,512,512]{3,2,1,0:T(8,128)(2,1)}, u32[]{:S(2)}) copy-start(bf16[2,1,512,512]{3,2,1,0:T(8,128)(2,1)} %param.32) | copy-start | bytes 3145732
  7.2 8.9 %copy-start.22 = (bf16[1,512,512]{2,1,0:T(8,128)(2,1)S(1)}, bf16[1,512,512]{2,1,0:T(8,128)(2,1)}, u32[]{:S(2)}) copy-start(bf16[1,512,512]{2,1,0:T(8,128)(2,1)} %param.39) | copy-start | bytes 1572868
  7.2 8.9 %copy-start.53 = (s32[2,1,512]{2,1,0:T(1,128)S(1)}, s32[2,1,512]{2,1,0:T(1,128)}, u32[]{:S(2)}) copy-start(s32[2,1,512]{2,1,0:T(1,128)} %param.34) | copy-start | bytes 12292
  7.2 8.9 %copy-start.89 = (f32[1,512]{1,0:T(1,128)S(1)}, f32[1,512]{1,0:T(1,128)}, u32[]{:S(2)}) copy-start(f32[1,512]{1,0:T(1,128)} %param.35) | copy-start | bytes 6148
  7.2 8.9 %copy-start.79 = (f32[1,512]{1,0:T(1,128)S(1)}, f32[1,512]{1,0:T(1,128)}, u32[]{:S(2)}) copy-start(f32[1,512]{1,0:T(1,128)} %param.36) | copy-start | bytes 6148
  7.2 8.9 %copy-start.52 = (f32[1,1536]{1,0:T(1,128)S(1)}, f32[1,1536]{1,0:T(1,128)}, u32[]{:S(2)}) copy-start(f32[1,1536]{1,0:T(1,128)} %param.38) | copy-start | bytes 18436
  7.3 447.5 %reduce-scatter.2.cloned.1.call-start = ((), (), s32[]{:S(2)}) async-start(), calls=%async_computation.1 | async-start | bytes 81920 | tf_op jit(solution)/shard_map/reduce_scatter | solution.py:362
  7.3 7.4 %dynamic-slice-start = ((f32[2048]{0:T(1024)}, s32[]{:T(128)}), f32[1024]{0:T(1024)S(1)}, s32[]{:S(2)}) async-start(f32[2048]{0:T(1024)} %param.51, s32[]{:T(128)} %select_n.189), calls=%async_computation.13 | async-start | bytes 8704 | tf_op jit(solution)/shard_map/dynamic_slice | solution.py:263
  30.6 43.1 %collective-permute-start = (bf16[512,512]{1,0:T(8,128)(2,1)}, bf16[512,512]{1,0:T(8,128)(2,1)}, u32[]{:S(2)}, u32[]{:S(2)}) collective-permute-start(bf16[512,512]{1,0:T(8,128)(2,1)} %get-tuple-element.858), channel_id=1, source_target_pairs={{0,16},{1,17},{2,18},{3,19},{4,20},{5,21},{6,22},{7,23},{8,24},{9,... | collective-permute-start | bytes 1572872 | tf_op jit(solution)/shard_map/ppermute | solution.py:19
  82.5 10.0 %copy-start.56 = (s32[2,1,512]{2,1,0:T(1,128)S(1)}, s32[2,1,512]{2,1,0:T(1,128)}, u32[]{:S(2)}) copy-start(s32[2,1,512]{2,1,0:T(1,128)} %get-tuple-element.742) | copy-start | bytes 12292 | tf_op jit(solution)/shard_map/cond
  98.7 8.2 %copy-start.37 = (bf16[10,8,64]{2,1,0:T(8,128)(2,1)S(1)}, bf16[10,8,64]{2,1,0:T(8,128)(2,1)}, u32[]{:S(2)}) copy-start(bf16[10,8,64]{2,1,0:T(8,128)(2,1)} %get-tuple-element.1153) | copy-start | bytes 30724 | tf_op jit(solution)/shard_map/cond
  98.8 8.9 %copy-start.32 = (pred[512,522]{0,1:T(8,128)(4,1)S(1)}, pred[512,522]{0,1:T(8,128)(4,1)}, u32[]{:S(2)}) copy-start(pred[512,522]{0,1:T(8,128)(4,1)} %concatenate.111) | copy-start | bytes 801796 | tf_op jit(solution)/shard_map/cond
  107.7 6.5 %copy-start.62 = (f32[512]{0:T(512)S(1)}, f32[512]{0:T(512)}, u32[]{:S(2)}) copy-start(f32[512]{0:T(512)} %copy-done.61) | copy-start | bytes 6148 | tf_op jit(solution)/shard_map/cond
  107.7 6.5 %copy-start.66 = (f32[512]{0:T(512)S(1)}, f32[512]{0:T(512)}, u32[]{:S(2)}) copy-start(f32[512]{0:T(512)} %copy-done.65) | copy-start | bytes 6148 | tf_op jit(solution)/shard_map/cond
  107.7 6.6 %copy-start.68 = (bf16[512,2048]{1,0:T(8,128)(2,1)S(1)}, bf16[512,2048]{1,0:T(8,128)(2,1)}, u32[]{:S(2)}) copy-start(bf16[512,2048]{1,0:T(8,128)(2,1)} %get-tuple-element.749) | copy-start | bytes 6291460 | tf_op jit(solution)/shard_map/cond
  107.7 6.6 %copy-start.77 = (f32[1,2048]{1,0:T(1,128)S(1)}, f32[1,2048]{1,0:T(1,128)}, u32[]{:S(2)}) copy-start(f32[1,2048]{1,0:T(1,128)} %get-tuple-element.750) | copy-start | bytes 24580 | tf_op jit(solution)/shard_map/cond
  107.7 6.6 %copy-start.84 = (f32[1,512]{1,0:T(1,128)S(1)}, f32[1,512]{1,0:T(1,128)}, u32[]{:S(2)}) copy-start(f32[1,512]{1,0:T(1,128)} %get-tuple-element.748) | copy-start | bytes 6148 | tf_op jit(solution)/shard_map/cond
  107.7 6.6 %copy-start.94 = (f32[1,512]{1,0:T(1,128)S(1)}, f32[1,512]{1,0:T(1,128)}, u32[]{:S(2)}) copy-start(f32[1,512]{1,0:T(1,128)} %get-tuple-element.747) | copy-start | bytes 6148 | tf_op jit(solution)/shard_map/cond
  117.8 10.9 %copy-start.81 = (f32[1,512]{1,0:T(1,128)S(1)}, f32[1,512]{1,0:T(1,128)}, u32[]{:S(2)}) copy-start(f32[1,512]{1,0:T(1,128)} %get-tuple-element.746) | copy-start | bytes 6148 | tf_op jit(solution)/shard_map/cond
  117.8 10.9 %copy-start.87 = (f32[1,512]{1,0:T(1,128)S(1)}, f32[1,512]{1,0:T(1,128)}, u32[]{:S(2)}) copy-start(f32[1,512]{1,0:T(1,128)} %get-tuple-element.752) | copy-start | bytes 6148 | tf_op jit(solution)/shard_map/cond
  130.0 4.1 collective-permute-start.1
  143.0 8.7 %copy-start.57 = (s32[2,1,512]{2,1,0:T(1,128)S(1)}, s32[2,1,512]{2,1,0:T(1,128)}, u32[]{:S(2)}) copy-start(s32[2,1,512]{2,1,0:T(1,128)} %get-tuple-element.759) | copy-start | bytes 12292 | tf_op jit(solution)/shard_map/cond
  145.6 6.5 %copy-start.41 = (bf16[10,8,64]{2,1,0:T(8,128)(2,1)S(1)}, bf16[10,8,64]{2,1,0:T(8,128)(2,1)}, u32[]{:S(2)}) copy-start(bf16[10,8,64]{2,1,0:T(8,128)(2,1)} %get-tuple-element.1173) | copy-start | bytes 30724 | tf_op jit(solution)/shard_map/cond
  161.7 6.5 %copy-start.69 = (bf16[512,2048]{1,0:T(8,128)(2,1)S(1)}, bf16[512,2048]{1,0:T(8,128)(2,1)}, u32[]{:S(2)}) copy-start(bf16[512,2048]{1,0:T(8,128)(2,1)} %get-tuple-element.766) | copy-start | bytes 6291460 | tf_op jit(solution)/shard_map/cond
  161.7 6.5 %copy-start.78 = (f32[1,2048]{1,0:T(1,128)S(1)}, f32[1,2048]{1,0:T(1,128)}, u32[]{:S(2)}) copy-start(f32[1,2048]{1,0:T(1,128)} %get-tuple-element.767) | copy-start | bytes 24580 | tf_op jit(solution)/shard_map/cond
  161.7 6.5 %copy-start.85 = (f32[1,512]{1,0:T(1,128)S(1)}, f32[1,512]{1,0:T(1,128)}, u32[]{:S(2)}) copy-start(f32[1,512]{1,0:T(1,128)} %get-tuple-element.765) | copy-start | bytes 6148 | tf_op jit(solution)/shard_map/cond
  161.7 6.5 %copy-start.95 = (f32[1,512]{1,0:T(1,128)S(1)}, f32[1,512]{1,0:T(1,128)}, u32[]{:S(2)}) copy-start(f32[1,512]{1,0:T(1,128)} %get-tuple-element.764) | copy-start | bytes 6148 | tf_op jit(solution)/shard_map/cond
  171.6 10.9 %copy-start.23 = (bf16[512,512]{1,0:T(8,128)(2,1)S(1)}, bf16[512,512]{1,0:T(8,128)(2,1)}, u32[]{:S(2)}) copy-start(bf16[512,512]{1,0:T(8,128)(2,1)} %get-tuple-element.762) | copy-start | bytes 1572868 | tf_op jit(solution)/shard_map/cond
  171.6 10.9 %copy-start.82 = (f32[1,512]{1,0:T(1,128)S(1)}, f32[1,512]{1,0:T(1,128)}, u32[]{:S(2)}) copy-start(f32[1,512]{1,0:T(1,128)} %get-tuple-element.763) | copy-start | bytes 6148 | tf_op jit(solution)/shard_map/cond
  171.6 10.9 %copy-start.88 = (f32[1,512]{1,0:T(1,128)S(1)}, f32[1,512]{1,0:T(1,128)}, u32[]{:S(2)}) copy-start(f32[1,512]{1,0:T(1,128)} %get-tuple-element.769) | copy-start | bytes 6148 | tf_op jit(solution)/shard_map/cond
  187.5 12.1 %copy-start.48 = (f32[2,8,512]{2,1,0:T(8,128)}, f32[2,8,512]{2,1,0:T(8,128)S(1)}, u32[]{:S(2)}) copy-start(f32[2,8,512]{2,1,0:T(8,128)S(1)} %pad_maximum_fusion.23) | copy-start | bytes 98308
  216.4 8.7 %slice-start.6 = ((s8[8650752]{0:T(1024)(128)(4,1)}), s8[262144]{0:T(1024)(128)(4,1)S(1)}, s32[]{:S(2)}) async-start(s8[8650752]{0:T(1024)(128)(4,1)} %bitcast.590), calls=%async_computation.8 | async-start | bytes 524288 | tf_op jit(solution)/shard_map/cond
  218.0 7.1 %slice-start.7 = ((s8[8650752]{0:T(1024)(128)(4,1)}), s8[4194304]{0:T(1024)(128)(4,1)S(1)}, s32[]{:S(2)}) async-start(s8[8650752]{0:T(1024)(128)(4,1)} %bitcast.590), calls=%async_computation.9 | async-start | bytes 8388608 | tf_op jit(solution)/shard_map/cond
  218.0 7.1 %slice-start.8 = ((s8[8650752]{0:T(1024)(128)(4,1)}), s8[4194304]{0:T(1024)(128)(4,1)S(1)}, s32[]{:S(2)}) async-start(s8[8650752]{0:T(1024)(128)(4,1)} %bitcast.590), calls=%async_computation.10 | async-start | bytes 8388608 | tf_op jit(solution)/shard_map/cond
  218.0 7.1 %copy-start.18 = (pred[512,522]{0,1:T(8,128)(4,1)S(1)}, pred[512,522]{0,1:T(8,128)(4,1)}, u32[]{:S(2)}) copy-start(pred[512,522]{0,1:T(8,128)(4,1)} %concatenate.121) | copy-start | bytes 801796 | tf_op jit(solution)/shard_map/cond
  277.2 6.1 %collective-permute-start.2 = (bf16[512,512]{0,1:T(8,128)(2,1)}, bf16[512,512]{0,1:T(8,128)(2,1)}, u32[]{:S(2)}, u32[]{:S(2)}) collective-permute-start(bf16[512,512]{0,1:T(8,128)(2,1)} %convert_element_type.543), channel_id=1, source_target_pairs={{16,0},{17,1},{18,2},{19,3},{20,4},{21,5},{22,6},{23,7},{24,8},{25... | collective-permute-start | bytes 1572872 | tf_op jit(solution)/shard_map/ppermute | solution.py:19
  286.5 6.8 %copy-start.58 = (s32[2,1,512]{2,1,0:T(1,128)S(1)}, s32[2,1,512]{2,1,0:T(1,128)}, u32[]{:S(2)}) copy-start(s32[2,1,512]{2,1,0:T(1,128)} %get-tuple-element.800) | copy-start | bytes 12292 | tf_op jit(solution)/shard_map/cond
  286.5 7.9 %copy-start.50 = (f32[2,8,512]{2,1,0:T(8,128)S(1)}, f32[2,8,512]{2,1,0:T(8,128)}, u32[]{:S(2)}) copy-start(f32[2,8,512]{2,1,0:T(8,128)} %get-tuple-element.802) | copy-start | bytes 98308 | tf_op jit(solution)/shard_map/cond
  299.6 8.7 %slice-start.3 = ((s8[8650752]{0:T(1024)(128)(4,1)}), s8[262144]{0:T(1024)(128)(4,1)S(1)}, s32[]{:S(2)}) async-start(s8[8650752]{0:T(1024)(128)(4,1)} %bitcast.588), calls=%async_computation.5 | async-start | bytes 524288 | tf_op jit(solution)/shard_map/cond
  301.2 7.1 %slice-start.4 = ((s8[8650752]{0:T(1024)(128)(4,1)}), s8[4194304]{0:T(1024)(128)(4,1)S(1)}, s32[]{:S(2)}) async-start(s8[8650752]{0:T(1024)(128)(4,1)} %bitcast.588), calls=%async_computation.6 | async-start | bytes 8388608 | tf_op jit(solution)/shard_map/cond
  301.2 7.1 %slice-start.5 = ((s8[8650752]{0:T(1024)(128)(4,1)}), s8[4194304]{0:T(1024)(128)(4,1)S(1)}, s32[]{:S(2)}) async-start(s8[8650752]{0:T(1024)(128)(4,1)} %bitcast.588), calls=%async_computation.7 | async-start | bytes 8388608 | tf_op jit(solution)/shard_map/cond
  301.2 7.1 %copy-start.17 = (pred[512,522]{0,1:T(8,128)(4,1)S(1)}, pred[512,522]{0,1:T(8,128)(4,1)}, u32[]{:S(2)}) copy-start(pred[512,522]{0,1:T(8,128)(4,1)} %concatenate.126) | copy-start | bytes 801796 | tf_op jit(solution)/shard_map/cond
  360.6 9.6 %collective-permute-start.3 = (bf16[512,512]{0,1:T(8,128)(2,1)}, bf16[512,512]{0,1:T(8,128)(2,1)}, u32[]{:S(2)}, u32[]{:S(2)}) collective-permute-start(bf16[512,512]{0,1:T(8,128)(2,1)} %convert_element_type.545), channel_id=1, source_target_pairs={{16,0},{17,1},{18,2},{19,3},{20,4},{21,5},{22,6},{23,7},{24,8},{25... | collective-permute-start | bytes 1572872 | tf_op jit(solution)/shard_map/ppermute | solution.py:19
  362.7 7.5 %copy-start.40 = (bf16[10,8,64]{2,1,0:T(8,128)(2,1)S(1)}, bf16[10,8,64]{2,1,0:T(8,128)(2,1)}, u32[]{:S(2)}) copy-start(bf16[10,8,64]{2,1,0:T(8,128)(2,1)} %reshape.734) | copy-start | bytes 30724
  362.7 7.5 %copy-start.49 = (f32[2,8,512]{2,1,0:T(8,128)S(1)}, f32[2,8,512]{2,1,0:T(8,128)}, u32[]{:S(2)}) copy-start(f32[2,8,512]{2,1,0:T(8,128)} %copy-done.48) | copy-start | bytes 98308
  362.7 7.5 %copy-start.55 = (s32[2,1,512]{2,1,0:T(1,128)S(1)}, s32[2,1,512]{2,1,0:T(1,128)}, u32[]{:S(2)}) copy-start(s32[2,1,512]{2,1,0:T(1,128)} %param.34) | copy-start | bytes 12292
  376.3 94.0 %copy-start.28 = (f32[10,512]{1,0:T(8,128)S(1)}, f32[10,512]{1,0:T(8,128)}, u32[]{:S(2)}) copy-start(f32[10,512]{1,0:T(8,128)} %copy-done.27) | copy-start | bytes 61444
  376.3 128.4 %copy-start.51 = (f32[10,512]{1,0:T(8,128)S(1)}, f32[10,512]{1,0:T(8,128)}, u32[]{:S(2)}) copy-start(f32[10,512]{1,0:T(8,128)} %param.47) | copy-start | bytes 61444
  (35 other events, 106.9 us)
Sparse Core Ops, SparseCore 0:
  376.5 78.2 reduce-scatter.1
where the time goes:
time: 522 us; the launch traced here: 517 us
  matrix products  158 us (30%)
  waiting for transfers between devices  120 us (23%)
  local copies, waits for them, and re-layouts  89.4 us (17%)
  other arithmetic  68.3 us (13%)
  blocking collectives  47 us (9%)
  between operations  14.6 us (3%)
  loops' own time  13.2 us (3%)
  starting transfers between devices  6.84 us (1%)
    reduce_scatter x1, waiting for transfers between devices, local(): lax.psum_scatter(prefix_total, 'dp', scatter_dimension=1, tiled=True)  75 us
    ppermute x4, waiting for transfers between devices, passed_along(): return lax.ppermute(shard, axis, pairs)  44.6 us
    dot_general x2, matrix products, backward_layer(): jnp.dot(grad_before, w_in.T, preferred_element_type=jnp.float32)  33 us
    psum x1, blocking collectives, local(): hidden_grad = lax.psum(hidden_part, ('pipe', 'dp'))  31.4 us
    another operation x21, local copies, waits for them, and re-layouts  22.9 us
    dot_general x2, matrix products, forward_layer(): jnp.dot(activated, w_back, preferred_element_type=jnp.float32)  21.8 us
    psum x1, blocking collectives, local(): local_cols = lax.psum(local_cols, 'grp')  15.6 us
    cond x118, local copies, waits for them, and re-layouts  15.1 us
  transfers between devices with their start and end apart: 5, of which 3 were waited for; matrix products, arithmetic and copies ran while one was open for 3% of the time, Pallas kernels for 0%

commit v1 on v0

--- a/solution.py
+++ b/solution.py
@@ -360,7 +360,11 @@
     dp_index = lax.axis_index("dp")
     col_width = 2 * D // lax.axis_size("dp")
     local_cols = lax.psum_scatter(prefix_total, "dp", scatter_dimension=1, tiled=True)
-    local_cols = lax.psum(local_cols, "grp")
+    local_cols = local_cols
+    for hop in (1, 2):
+        local_cols = local_cols + lax.ppermute(
+            local_cols, "grp", [(dev, dev ^ hop) for dev in range(4)]
+        )
     grad_out_weight = matmul_hi(hidden_units.T, local_cols)
     grad_out_bias = jnp.sum(local_cols, axis=0)
     out_cols = lax.dynamic_slice_in_dim(

time: 522 us -> 509 us (0.975)
  blocking collectives: 47 us -> 29.9 us
    psum x1 -> x0, blocking collectives: 15.6 us -> none  [local(): local_cols = lax.psum(local_cols, 'grp')]
  transfers between devices with their start and end apart: 5 -> 7, of which waited for: 3 -> 4; matrix products, arithmetic and copies ran while one was open for 3% -> 3% of each run, Pallas kernels for 0% -> 0%
where the time goes in v1:
time: 509 us; the launch traced here: 503 us
  matrix products  158 us (31%)
  waiting for transfers between devices  120 us (24%)
  local copies, waits for them, and re-layouts  87.9 us (17%)
  other arithmetic  69.1 us (14%)
  blocking collectives  29.9 us (6%)
  between operations  14.6 us (3%)
  loops' own time  13.5 us (3%)
  starting transfers between devices  10.1 us (2%)
    reduce_scatter x1, waiting for transfers between devices, local(): lax.psum_scatter(prefix_total, 'dp', scatter_dimension=1, tiled=True)  74.4 us
    ppermute x4, waiting for transfers between devices, passed_along(): return lax.ppermute(shard, axis, pairs)  44.6 us
    dot_general x2, matrix products, backward_layer(): jnp.dot(grad_before, w_in.T, preferred_element_type=jnp.float32)  33 us
    psum x1, blocking collectives, local(): hidden_grad = lax.psum(hidden_part, ('pipe', 'dp'))  29.9 us
    another operation x21, local copies, waits for them, and re-layouts  22.7 us
    dot_general x2, matrix products, forward_layer(): jnp.dot(activated, w_back, preferred_element_type=jnp.float32)  21.8 us
    cond x118, local copies, waits for them, and re-layouts  15 us
    another operation x9, other arithmetic, local(): jnp.stack(leaf_list)  14.7 us
  transfers between devices with their start and end apart: 7, of which 4 were waited for; matrix products, arithmetic and copies ran while one was open for 3% of the time, Pallas kernels for 0%

profile of v1, /device:TPU:1, one launch (start us, length us, event | category | flops | bytes accessed | tf_op | source)
XLA Modules:
  0.0 503.4 jit_solution(17883562240558342991)
XLA Ops:
  10.4 4.3 fusion.607
  16.2 14.3 %conditional.6 = (bf16[512,512]{1,0:T(8,128)(2,1)}, bf16[512,8,64]{0,2,1:T(8,128)(2,1)}, bf16[512,8,64]{0,2,1:T(8,128)(2,1)}, bf16[512,8,64]{0,2,1:T(8,128)(2,1)...) conditional(s32[]{:T(128)} %convert_element_type.537, () %tuple.74, (bf16[512,512]{1,0:T(8,128)(2,1)S(1)}, ...), branch_computations={%region_0.1_spmd, %region_1.6_spmd} | conditional | flops 3878450176 | bytes 134584976 | solution.py:295
  16.2 2.5 broadcast.1317
  31.8 41.8 %collective-permute-done = bf16[512,512]{1,0:T(8,128)(2,1)} collective-permute-done((bf16[512,512]{1,0:T(8,128)(2,1)}, bf16[512,512]{1,0:T(8,128)(2,1)}, u32[]{:S(2)}, u32[]{:S(2)}) %collective-permute-start) | collective-permute-done | bytes 524320 | tf_op jit(solution)/shard_map/ppermute | solution.py:19
  75.5 54.5 %conditional.7 = (bf16[512,512]{1,0:T(8,128)(2,1)}, bf16[512,8,64]{0,2,1:T(8,128)(2,1)}, bf16[512,8,64]{0,2,1:T(8,128)(2,1)}, bf16[512,8,64]{0,2,1:T(8,128)(2,1)...) conditional(s32[]{:T(128)} %convert_element_type.539, () %tuple.76, (bf16[512,512]{1,0:T(8,128)(2,1)S(1)}, ...), branch_computations={%region_6.7_spmd, %region_7.12_spmd} | conditional | flops 3878450176 | bytes 134601392 | solution.py:295
  76.7 2.5 convolution_add_fusion.3
  82.4 2.5 copy.118
  85.0 2.5 copy.119
  95.0 3.6 fusion.419
  107.7 6.5 %fusion.437 = bf16[8,64,512]{2,1,0:T(8,128)(2,1)S(1)} fusion(f32[8,512,522]{1,2,0:T(8,128)} %copy-done.4, f32[8,512]{1,0:T(8,128)S(1)} %fusion.420, f32[8,512]{1,0:T(8,128)S(1)} %get-tuple-element.1338, pred[512,522]{0,1:T(8,128)(4,1)S(1)} %copy-done.33, bf16[512,8,64]{0,2,1:T(8,128)(2,1)} %bitcast.15, bf16[10,8,64]{0,2,1:T(8,128)(2,1)} %copy.131), kind=kOutput, calls=%fused_computation.587 | convolution fusion | flops 285700096 | bytes 9911296 | tf_op jit(solution)/shard_map/cond/branch_1_fun/hqk,khd->qhd/dot_general | solution.py:76
  114.3 3.5 convolution_add_fusion.4
  117.7 10.9 %fusion.432 = f32[512,512]{1,0:T(8,128)S(1)} fusion(bf16[2048,512]{1,0:T(8,128)(2,1)S(1)} %copy-done.73, f32[512,2048]{1,0:T(8,128)} %convolution_add_fusion.4), kind=kOutput, calls=%fused_computation.579 | convolution fusion | flops 1141899264 | bytes 7340032 | tf_op jit(solution)/shard_map/cond/branch_1_fun/dot_general | solution.py:153
  131.3 2.8 collective-permute-done.1
  136.1 47.8 %conditional.8 = (bf16[512,512]{1,0:T(8,128)(2,1)}, bf16[512,8,64]{0,2,1:T(8,128)(2,1)}, bf16[512,8,64]{0,2,1:T(8,128)(2,1)}, bf16[512,8,64]{0,2,1:T(8,128)(2,1)...) conditional(s32[]{:T(128)} %convert_element_type.540, () %tuple.78, (bf16[512,512]{1,0:T(8,128)(2,1)S(1)}, ...), branch_computations={%region_12.13_spmd, %region_13.18_spmd} | conditional | flops 3878450176 | bytes 134044168 | solution.py:295
  137.7 2.5 convolution_add_fusion.6
  143.0 2.5 copy.121
  152.3 3.4 fusion.503
  161.7 6.4 %fusion.521 = bf16[8,64,512]{2,1,0:T(8,128)(2,1)S(1)} fusion(f32[8,512,522]{1,2,0:T(8,128)} %copy-done.5, f32[8,512]{1,0:T(8,128)S(1)} %fusion.504, f32[8,512]{1,0:T(8,128)S(1)} %get-tuple-element.1352, pred[512,522]{0,1:T(8,128)(4,1)S(1)} %concatenate.116, bf16[512,8,64]{0,2,1:T(8,128)(2,1)} %bitcast.28, bf16[10,8,64]{0,2,1:T(8,128)(2,1)S(1)} %copy.133), kind=kOutput, calls=%fused_computation.704 | convolution fusion | flops 285700096 | bytes 9911296 | tf_op jit(solution)/shard_map/cond/branch_1_fun/hqk,khd->qhd/dot_general | solution.py:76
  168.1 3.4 convolution_add_fusion.7
  171.5 10.9 %fusion.516 = f32[512,512]{1,0:T(8,128)S(1)} fusion(bf16[2048,512]{1,0:T(8,128)(2,1)S(1)} %copy-done.74, f32[512,2048]{1,0:T(8,128)} %convolution_add_fusion.7), kind=kOutput, calls=%fused_computation.696 | convolution fusion | flops 1141899264 | bytes 7340032 | tf_op jit(solution)/shard_map/cond/branch_1_fun/dot_general | solution.py:153
  189.9 4.8 select_bitcast_fusion.1
  194.7 3.9 pad_maximum_fusion.18
  199.5 75.5 %conditional.9 = (f32[512,512]{0,1:T(8,128)}, f32[10,1024]{1,0:T(8,128)}) conditional(s32[]{:T(128)} %convert_element_type.541, () %tuple.80, (bf16[2,1,512,512]{3,2,1,0:T(8,128)(2,1)}, pred[512,512]{1,0:T(32,128)(4,1)}, bf16[]{:T(256)}, s32[]{:T(128)}, f32[2,512,2048]{2,1,0:T(8,128)}, /*index=5*/bf16[2048,512]{1,0:T(8,128)(2,1)}, ...), branch_computations={%region_18.19_spmd, %region_19.27_spmd} | conditional | flops 4719746048 | bytes 179329520 | solution.py:347
  199.6 2.3 dynamic-slice_bitcast_fusion
  202.0 6.8 %fusion.63 = f32[8,512,522]{1,2,0:T(8,128)} fusion(bf16[2,512,8,64]{1,3,2,0:T(8,128)(2,1)S(1)} %get-tuple-element.782, s32[]{:T(128)S(6)} %min.25, bf16[512,8,64]{0,2,1:T(8,128)(2,1)} %get-tuple-element.1281, bf16[10,8,64]{0,2,1:T(8,128)(2,1)S(1)} %copy.138), kind=kOutput, calls=%fused_computation.79 | convolution fusion | flops 274747392 | bytes 9732100 | tf_op jit(solution)/shard_map/cond/branch_1_fun/qhd,khd->hqk/dot_general | solution.py:94
  209.9 2.5 copy.135
  213.7 2.6 convolution_convert_fusion
  217.9 7.1 %multiply_reduce_fusion = (f32[8,512]{1,0:T(8,128)S(1)}, f32[8,512,522]{1,2,0:T(8,128)S(1)}) fusion(f32[8,512,522]{1,2,0:T(8,128)} %fusion.63, f32[8,512]{1,0:T(8,128)S(1)} %dynamic-slice_bitcast_fusion.2, pred[512,522]{0,1:T(8,128)(4,1)} %concatenate.121, bf16[512,8,64]{0,2,1:T(8,128)(2,1)} %bitcast.620, bf16[512,8,64]{0,2,1:T(8,128)(2,1)} %get-tuple-element.1280, ...), kind=kOutput, calls=%fused_computation.1 | convolution fusion | flops 285433856 | bytes 18463744 | tf_op jit(solution)/shard_map/cond/branch_1_fun/qhd,khd->hqk/dot_general | solution.py:103
  225.0 2.7 multiply_convert_fusion
  233.1 5.4 %fusion.37 = f32[522,8,64]{0,2,1:T(8,128)S(1)} fusion(bf16[512,8,64]{0,2,1:T(8,128)(2,1)} %bitcast.621, f32[8,512,522]{1,2,0:T(8,128)} %fusion.63, f32[8,512]{1,0:T(8,128)S(1)} %dynamic-slice_bitcast_fusion.2, pred[512,522]{0,1:T(8,128)(4,1)} %concatenate.121), kind=kOutput, calls=%fused_computation.48 | convolution fusion | flops 282230784 | bytes 10429440 | tf_op jit(solution)/shard_map/cond/branch_1_fun/hqk,qhd->khd/dot_general | solution.py:100
  241.9 3.4 fusion.40
  252.7 16.5 %fusion.54 = (f32[512]{0:T(512)S(1)}, f32[512]{0:T(512)S(1)}, f32[512]{0:T(512)S(1)}, f32[512,512]{0,1:T(8,128)}) fusion(f32[512]{0:T(512)S(1)} %broadcast_multiply_fusion, bf16[2,512,512]{1,2,0:T(8,128)(2,1)} %copy.137, s32[]{:T(128)S(6)} %min.25, f32[512,512]{0,1:T(8,128)} %fusion.41, f32[512]{0:T(512)S(1)} %bitcast.679, ...), kind=kOutput, calls=%fused_computation.63 | convolution fusion | flops 2225601024 | bytes 11808256 | tf_op jit(solution)/shard_map/cond/branch_1_fun/dot_general | solution.py:180
  271.3 3.5 add_add_fusion.2
  283.1 75.1 %conditional.10 = (f32[512,512]{0,1:T(8,128)}, f32[10,1024]{1,0:T(8,128)}) conditional(s32[]{:T(128)} %convert_element_type.542, () %tuple.82, (pred[512,512]{1,0:T(32,128)(4,1)}, bf16[512,512]{0,1:T(8,128)(2,1)}, bf16[512,512]{0,1:T(8,128)(2,1)}, s32[]{:T(128)}, f32[2,512,2048]{2,1,0:T(8,128)}, /*index=5*/bf16[2048,512]{1,0:T(8,128)(2,1)}, ...), branch_computations={%region_27.28_spmd, %region_28.36_spmd} | conditional | flops 4719221760 | bytes 178427408 | solution.py:347
  286.3 6.8 %fusion.179 = f32[8,512,522]{1,2,0:T(8,128)} fusion(bf16[2,512,8,64]{1,3,2,0:T(8,128)(2,1)S(1)} %get-tuple-element.801, s32[]{:T(128)S(6)} %min.26, bf16[512,8,64]{0,2,1:T(8,128)(2,1)} %get-tuple-element.1297, bf16[10,8,64]{0,2,1:T(8,128)(2,1)S(1)} %copy.143), kind=kOutput, calls=%fused_computation.224 | convolution fusion | flops 274747392 | bytes 9732100 | tf_op jit(solution)/shard_map/cond/branch_1_fun/qhd,khd->hqk/dot_general | solution.py:94
  296.9 2.5 convolution_convert_fusion.1
  301.0 7.1 %multiply_reduce_fusion.1 = (f32[8,512]{1,0:T(8,128)S(1)}, f32[8,512,522]{1,2,0:T(8,128)S(1)}) fusion(f32[8,512,522]{1,2,0:T(8,128)} %fusion.179, f32[8,512]{1,0:T(8,128)S(1)} %dynamic-slice_bitcast_fusion.5, pred[512,522]{0,1:T(8,128)(4,1)} %concatenate.126, bf16[512,8,64]{0,2,1:T(8,128)(2,1)} %bitcast.613, bf16[512,8,64]{0,2,1:T(8,128)(2,1)} %get-tuple-element.1296, ...), kind=kOutput, calls=%fused_computation.148 | convolution fusion | flops 285433856 | bytes 18463744 | tf_op jit(solution)/shard_map/cond/branch_1_fun/qhd,khd->hqk/dot_general | solution.py:103
  308.1 2.9 multiply_convert_fusion.1
  316.4 5.4 %fusion.154 = f32[522,8,64]{0,2,1:T(8,128)S(1)} fusion(bf16[512,8,64]{0,2,1:T(8,128)(2,1)} %bitcast.614, f32[8,512,522]{1,2,0:T(8,128)} %fusion.179, f32[8,512]{1,0:T(8,128)S(1)} %dynamic-slice_bitcast_fusion.5, pred[512,522]{0,1:T(8,128)(4,1)} %concatenate.126), kind=kOutput, calls=%fused_computation.195 | convolution fusion | flops 282230784 | bytes 10429440 | tf_op jit(solution)/shard_map/cond/branch_1_fun/hqk,qhd->khd/dot_general | solution.py:100
  325.1 3.4 fusion.157
  335.8 16.5 %fusion.171 = (f32[512]{0:T(512)S(1)}, f32[512]{0:T(512)S(1)}, f32[512]{0:T(512)S(1)}, f32[512,512]{0,1:T(8,128)}) fusion(f32[512]{0:T(512)S(1)} %broadcast_multiply_fusion.1, bf16[2,512,512]{1,2,0:T(8,128)(2,1)} %copy.142, s32[]{:T(128)S(6)} %min.26, f32[512,512]{0,1:T(8,128)} %fusion.158, f32[512]{0:T(512)S(1)} %bitcast.680, ...), kind=kOutput, calls=%fused_computation.210 | convolution fusion | flops 2225338880 | bytes 11545600 | tf_op jit(solution)/shard_map/cond/branch_1_fun/dot_general | solution.py:180
  352.3 2.6 fusion.181
  354.9 3.3 add_add_fusion.5
  362.4 2.5 copy.145
  367.2 4.8 conditional.11
  373.6 2.3 maximum_bitcast_fusion.1
  377.5 74.4 %reduce-scatter.2.cloned.1.call-done = f32[10,256]{1,0:T(8,128)} async-done(((f32[10,1024]{1,0:T(8,128)}), f32[10,256]{1,0:T(8,128)}) %reduce-scatter.2.cloned.1.call-update) | async-done | bytes 10256 | tf_op jit(solution)/shard_map/reduce_scatter | solution.py:362
  459.9 29.9 %psum.7 = f32[10,512]{1,0:T(8,128)S(1)} all-reduce(f32[10,512]{1,0:T(8,128)S(1)} %fusion.588), channel_id=1, replica_groups=mesh['pipe'=2,'grp'=4,'dp'=4] {'pipe','dp'}, use_global_device_ids=true, to_apply=%region_46.47 | all-reduce | flops 5120 | bytes 40960 | tf_op jit(solution)/shard_map/psum | solution.py:374
  (323 shorter events, 141.5 us)
Async XLA Ops:
  7.2 8.9 %copy-start.15 = (bf16[2,1,512,512]{3,2,1,0:T(8,128)(2,1)S(1)}, bf16[2,1,512,512]{3,2,1,0:T(8,128)(2,1)}, u32[]{:S(2)}) copy-start(bf16[2,1,512,512]{3,2,1,0:T(8,128)(2,1)} %param.32) | copy-start | bytes 3145732
  7.2 8.9 %copy-start.23 = (bf16[1,512,512]{2,1,0:T(8,128)(2,1)S(1)}, bf16[1,512,512]{2,1,0:T(8,128)(2,1)}, u32[]{:S(2)}) copy-start(bf16[1,512,512]{2,1,0:T(8,128)(2,1)} %param.39) | copy-start | bytes 1572868
  7.2 8.9 %copy-start.54 = (s32[2,1,512]{2,1,0:T(1,128)S(1)}, s32[2,1,512]{2,1,0:T(1,128)}, u32[]{:S(2)}) copy-start(s32[2,1,512]{2,1,0:T(1,128)} %param.34) | copy-start | bytes 12292
  7.2 8.9 %copy-start.91 = (f32[1,512]{1,0:T(1,128)S(1)}, f32[1,512]{1,0:T(1,128)}, u32[]{:S(2)}) copy-start(f32[1,512]{1,0:T(1,128)} %param.35) | copy-start | bytes 6148
  7.2 8.9 %copy-start.81 = (f32[1,512]{1,0:T(1,128)S(1)}, f32[1,512]{1,0:T(1,128)}, u32[]{:S(2)}) copy-start(f32[1,512]{1,0:T(1,128)} %param.36) | copy-start | bytes 6148
  7.2 8.9 %copy-start.53 = (f32[1,1536]{1,0:T(1,128)S(1)}, f32[1,1536]{1,0:T(1,128)}, u32[]{:S(2)}) copy-start(f32[1,1536]{1,0:T(1,128)} %param.38) | copy-start | bytes 18436
  7.3 444.6 %reduce-scatter.2.cloned.1.call-start = ((), (), s32[]{:S(2)}) async-start(), calls=%async_computation.1 | async-start | bytes 81920 | tf_op jit(solution)/shard_map/reduce_scatter | solution.py:362
  7.3 7.4 %dynamic-slice-start = ((f32[2048]{0:T(1024)}, s32[]{:T(128)}), f32[1024]{0:T(1024)S(1)}, s32[]{:S(2)}) async-start(f32[2048]{0:T(1024)} %param.51, s32[]{:T(128)} %select_n.189), calls=%async_computation.13 | async-start | bytes 8704 | tf_op jit(solution)/shard_map/dynamic_slice | solution.py:263
  30.5 43.1 %collective-permute-start = (bf16[512,512]{1,0:T(8,128)(2,1)}, bf16[512,512]{1,0:T(8,128)(2,1)}, u32[]{:S(2)}, u32[]{:S(2)}) collective-permute-start(bf16[512,512]{1,0:T(8,128)(2,1)} %get-tuple-element.858), channel_id=1, source_target_pairs={{0,16},{1,17},{2,18},{3,19},{4,20},{5,21},{6,22},{7,23},{8,24},{9,... | collective-permute-start | bytes 1572872 | tf_op jit(solution)/shard_map/ppermute | solution.py:19
  82.4 9.9 %copy-start.57 = (s32[2,1,512]{2,1,0:T(1,128)S(1)}, s32[2,1,512]{2,1,0:T(1,128)}, u32[]{:S(2)}) copy-start(s32[2,1,512]{2,1,0:T(1,128)} %get-tuple-element.742) | copy-start | bytes 12292 | tf_op jit(solution)/shard_map/cond
  98.7 8.2 %copy-start.38 = (bf16[10,8,64]{2,1,0:T(8,128)(2,1)S(1)}, bf16[10,8,64]{2,1,0:T(8,128)(2,1)}, u32[]{:S(2)}) copy-start(bf16[10,8,64]{2,1,0:T(8,128)(2,1)} %get-tuple-element.1153) | copy-start | bytes 30724 | tf_op jit(solution)/shard_map/cond
  98.7 9.0 %copy-start.33 = (pred[512,522]{0,1:T(8,128)(4,1)S(1)}, pred[512,522]{0,1:T(8,128)(4,1)}, u32[]{:S(2)}) copy-start(pred[512,522]{0,1:T(8,128)(4,1)} %concatenate.111) | copy-start | bytes 801796 | tf_op jit(solution)/shard_map/cond
  107.7 6.5 %copy-start.64 = (f32[512]{0:T(512)S(1)}, f32[512]{0:T(512)}, u32[]{:S(2)}) copy-start(f32[512]{0:T(512)} %copy-done.63) | copy-start | bytes 6148 | tf_op jit(solution)/shard_map/cond
  107.7 6.5 %copy-start.68 = (f32[512]{0:T(512)S(1)}, f32[512]{0:T(512)}, u32[]{:S(2)}) copy-start(f32[512]{0:T(512)} %copy-done.67) | copy-start | bytes 6148 | tf_op jit(solution)/shard_map/cond
  107.7 6.6 %copy-start.70 = (bf16[512,2048]{1,0:T(8,128)(2,1)S(1)}, bf16[512,2048]{1,0:T(8,128)(2,1)}, u32[]{:S(2)}) copy-start(bf16[512,2048]{1,0:T(8,128)(2,1)} %get-tuple-element.749) | copy-start | bytes 6291460 | tf_op jit(solution)/shard_map/cond
  107.7 6.6 %copy-start.79 = (f32[1,2048]{1,0:T(1,128)S(1)}, f32[1,2048]{1,0:T(1,128)}, u32[]{:S(2)}) copy-start(f32[1,2048]{1,0:T(1,128)} %get-tuple-element.750) | copy-start | bytes 24580 | tf_op jit(solution)/shard_map/cond
  107.7 6.6 %copy-start.86 = (f32[1,512]{1,0:T(1,128)S(1)}, f32[1,512]{1,0:T(1,128)}, u32[]{:S(2)}) copy-start(f32[1,512]{1,0:T(1,128)} %get-tuple-element.748) | copy-start | bytes 6148 | tf_op jit(solution)/shard_map/cond
  107.7 6.6 %copy-start.96 = (f32[1,512]{1,0:T(1,128)S(1)}, f32[1,512]{1,0:T(1,128)}, u32[]{:S(2)}) copy-start(f32[1,512]{1,0:T(1,128)} %get-tuple-element.747) | copy-start | bytes 6148 | tf_op jit(solution)/shard_map/cond
  117.7 10.9 %copy-start.83 = (f32[1,512]{1,0:T(1,128)S(1)}, f32[1,512]{1,0:T(1,128)}, u32[]{:S(2)}) copy-start(f32[1,512]{1,0:T(1,128)} %get-tuple-element.746) | copy-start | bytes 6148 | tf_op jit(solution)/shard_map/cond
  117.7 10.9 %copy-start.89 = (f32[1,512]{1,0:T(1,128)S(1)}, f32[1,512]{1,0:T(1,128)}, u32[]{:S(2)}) copy-start(f32[1,512]{1,0:T(1,128)} %get-tuple-element.752) | copy-start | bytes 6148 | tf_op jit(solution)/shard_map/cond
  130.0 4.1 collective-permute-start.1
  143.0 8.7 %copy-start.58 = (s32[2,1,512]{2,1,0:T(1,128)S(1)}, s32[2,1,512]{2,1,0:T(1,128)}, u32[]{:S(2)}) copy-start(s32[2,1,512]{2,1,0:T(1,128)} %get-tuple-element.759) | copy-start | bytes 12292 | tf_op jit(solution)/shard_map/cond
  145.5 6.6 %copy-start.42 = (bf16[10,8,64]{2,1,0:T(8,128)(2,1)S(1)}, bf16[10,8,64]{2,1,0:T(8,128)(2,1)}, u32[]{:S(2)}) copy-start(bf16[10,8,64]{2,1,0:T(8,128)(2,1)} %get-tuple-element.1173) | copy-start | bytes 30724 | tf_op jit(solution)/shard_map/cond
  161.6 6.5 %copy-start.80 = (f32[1,2048]{1,0:T(1,128)S(1)}, f32[1,2048]{1,0:T(1,128)}, u32[]{:S(2)}) copy-start(f32[1,2048]{1,0:T(1,128)} %get-tuple-element.767) | copy-start | bytes 24580 | tf_op jit(solution)/shard_map/cond
  171.5 10.9 %copy-start.24 = (bf16[512,512]{1,0:T(8,128)(2,1)S(1)}, bf16[512,512]{1,0:T(8,128)(2,1)}, u32[]{:S(2)}) copy-start(bf16[512,512]{1,0:T(8,128)(2,1)} %get-tuple-element.762) | copy-start | bytes 1572868 | tf_op jit(solution)/shard_map/cond
  171.5 10.9 %copy-start.84 = (f32[1,512]{1,0:T(1,128)S(1)}, f32[1,512]{1,0:T(1,128)}, u32[]{:S(2)}) copy-start(f32[1,512]{1,0:T(1,128)} %get-tuple-element.763) | copy-start | bytes 6148 | tf_op jit(solution)/shard_map/cond
  171.5 10.9 %copy-start.90 = (f32[1,512]{1,0:T(1,128)S(1)}, f32[1,512]{1,0:T(1,128)}, u32[]{:S(2)}) copy-start(f32[1,512]{1,0:T(1,128)} %get-tuple-element.769) | copy-start | bytes 6148 | tf_op jit(solution)/shard_map/cond
  187.4 12.1 %copy-start.49 = (f32[2,8,512]{2,1,0:T(8,128)}, f32[2,8,512]{2,1,0:T(8,128)S(1)}, u32[]{:S(2)}) copy-start(f32[2,8,512]{2,1,0:T(8,128)S(1)} %pad_maximum_fusion.23) | copy-start | bytes 98308
  216.3 8.7 %slice-start.6 = ((s8[8650752]{0:T(1024)(128)(4,1)}), s8[262144]{0:T(1024)(128)(4,1)S(1)}, s32[]{:S(2)}) async-start(s8[8650752]{0:T(1024)(128)(4,1)} %bitcast.588), calls=%async_computation.8 | async-start | bytes 524288 | tf_op jit(solution)/shard_map/cond
  217.9 7.1 %slice-start.7 = ((s8[8650752]{0:T(1024)(128)(4,1)}), s8[4194304]{0:T(1024)(128)(4,1)S(1)}, s32[]{:S(2)}) async-start(s8[8650752]{0:T(1024)(128)(4,1)} %bitcast.588), calls=%async_computation.9 | async-start | bytes 8388608 | tf_op jit(solution)/shard_map/cond
  217.9 7.1 %slice-start.8 = ((s8[8650752]{0:T(1024)(128)(4,1)}), s8[4194304]{0:T(1024)(128)(4,1)S(1)}, s32[]{:S(2)}) async-start(s8[8650752]{0:T(1024)(128)(4,1)} %bitcast.588), calls=%async_computation.10 | async-start | bytes 8388608 | tf_op jit(solution)/shard_map/cond
  217.9 7.2 %copy-start.19 = (pred[512,522]{0,1:T(8,128)(4,1)S(1)}, pred[512,522]{0,1:T(8,128)(4,1)}, u32[]{:S(2)}) copy-start(pred[512,522]{0,1:T(8,128)(4,1)} %concatenate.121) | copy-start | bytes 801796 | tf_op jit(solution)/shard_map/cond
  277.1 6.0 %collective-permute-start.2 = (bf16[512,512]{0,1:T(8,128)(2,1)}, bf16[512,512]{0,1:T(8,128)(2,1)}, u32[]{:S(2)}, u32[]{:S(2)}) collective-permute-start(bf16[512,512]{0,1:T(8,128)(2,1)} %convert_element_type.543), channel_id=1, source_target_pairs={{16,0},{17,1},{18,2},{19,3},{20,4},{21,5},{22,6},{23,7},{24,8},{25... | collective-permute-start | bytes 1572872 | tf_op jit(solution)/shard_map/ppermute | solution.py:19
  286.2 6.8 %copy-start.59 = (s32[2,1,512]{2,1,0:T(1,128)S(1)}, s32[2,1,512]{2,1,0:T(1,128)}, u32[]{:S(2)}) copy-start(s32[2,1,512]{2,1,0:T(1,128)} %get-tuple-element.800) | copy-start | bytes 12292 | tf_op jit(solution)/shard_map/cond
  286.2 7.9 %copy-start.51 = (f32[2,8,512]{2,1,0:T(8,128)S(1)}, f32[2,8,512]{2,1,0:T(8,128)}, u32[]{:S(2)}) copy-start(f32[2,8,512]{2,1,0:T(8,128)} %get-tuple-element.802) | copy-start | bytes 98308 | tf_op jit(solution)/shard_map/cond
  299.4 8.7 %slice-start.3 = ((s8[8650752]{0:T(1024)(128)(4,1)}), s8[262144]{0:T(1024)(128)(4,1)S(1)}, s32[]{:S(2)}) async-start(s8[8650752]{0:T(1024)(128)(4,1)} %bitcast.586), calls=%async_computation.5 | async-start | bytes 524288 | tf_op jit(solution)/shard_map/cond
  301.0 7.1 %slice-start.4 = ((s8[8650752]{0:T(1024)(128)(4,1)}), s8[4194304]{0:T(1024)(128)(4,1)S(1)}, s32[]{:S(2)}) async-start(s8[8650752]{0:T(1024)(128)(4,1)} %bitcast.586), calls=%async_computation.6 | async-start | bytes 8388608 | tf_op jit(solution)/shard_map/cond
  301.0 7.1 %slice-start.5 = ((s8[8650752]{0:T(1024)(128)(4,1)}), s8[4194304]{0:T(1024)(128)(4,1)S(1)}, s32[]{:S(2)}) async-start(s8[8650752]{0:T(1024)(128)(4,1)} %bitcast.586), calls=%async_computation.7 | async-start | bytes 8388608 | tf_op jit(solution)/shard_map/cond
  301.0 7.1 %copy-start.18 = (pred[512,522]{0,1:T(8,128)(4,1)S(1)}, pred[512,522]{0,1:T(8,128)(4,1)}, u32[]{:S(2)}) copy-start(pred[512,522]{0,1:T(8,128)(4,1)} %concatenate.126) | copy-start | bytes 801796 | tf_op jit(solution)/shard_map/cond
  358.2 9.0 %copy-start.41 = (bf16[10,8,64]{2,1,0:T(8,128)(2,1)S(1)}, bf16[10,8,64]{2,1,0:T(8,128)(2,1)}, u32[]{:S(2)}) copy-start(bf16[10,8,64]{2,1,0:T(8,128)(2,1)} %reshape.734) | copy-start | bytes 30724
  358.2 9.0 %copy-start.50 = (f32[2,8,512]{2,1,0:T(8,128)S(1)}, f32[2,8,512]{2,1,0:T(8,128)}, u32[]{:S(2)}) copy-start(f32[2,8,512]{2,1,0:T(8,128)} %copy-done.49) | copy-start | bytes 98308
  358.2 9.0 %copy-start.56 = (s32[2,1,512]{2,1,0:T(1,128)S(1)}, s32[2,1,512]{2,1,0:T(1,128)}, u32[]{:S(2)}) copy-start(s32[2,1,512]{2,1,0:T(1,128)} %param.34) | copy-start | bytes 12292
  360.4 6.8 %collective-permute-start.3 = (bf16[512,512]{0,1:T(8,128)(2,1)}, bf16[512,512]{0,1:T(8,128)(2,1)}, u32[]{:S(2)}, u32[]{:S(2)}) collective-permute-start(bf16[512,512]{0,1:T(8,128)(2,1)} %convert_element_type.545), channel_id=1, source_target_pairs={{16,0},{17,1},{18,2},{19,3},{20,4},{21,5},{22,6},{23,7},{24,8},{25... | collective-permute-start | bytes 1572872 | tf_op jit(solution)/shard_map/ppermute | solution.py:19
  372.0 81.1 %copy-start.16 = (f32[512,512]{1,0:T(8,128)S(1)}, f32[512,512]{1,0:T(8,128)}, u32[]{:S(2)}) copy-start(f32[512,512]{1,0:T(8,128)} %copy.145) | copy-start | bytes 3145732
  451.9 2.8 collective-permute-start.4
  453.1 36.7 %copy-start.29 = (f32[10,512]{1,0:T(8,128)S(1)}, f32[10,512]{1,0:T(8,128)}, u32[]{:S(2)}) copy-start(f32[10,512]{1,0:T(8,128)} %copy-done.28) | copy-start | bytes 61444
  453.1 36.7 %copy-start.52 = (f32[10,512]{1,0:T(8,128)S(1)}, f32[10,512]{1,0:T(8,128)}, u32[]{:S(2)}) copy-start(f32[10,512]{1,0:T(8,128)} %param.47) | copy-start | bytes 61444
  454.7 3.7 collective-permute-start.5
  (39 other events, 129.1 us)
Sparse Core Ops, SparseCore 0:
  373.8 78.0 reduce-scatter.1
